TPU v7x, 256 devices: a whole 4x4x8 slice. The times are simulated.
256 devices in a mesh: dp: 8 (over x, y_lo), fsdp: 16 (over z, core), tensor: 2 (over y_hi).
Axes of the slice: x: 4, y: 4 (y_hi: 2, y_lo: 2; y = y_hi * 2 + y_lo), z: 8, core: 2. Of those that a mesh axis runs over, the one named last changes fastest.
Arguments:
- pooled: bfloat16 [8, 3072, 1152], P('dp', 'fsdp'), may hold values from -6 to 6
- ln_gain: float32 [1152], replicated, may hold values from 0.5 to 1.5
- w_in: bfloat16 [1152, 4304], P('fsdp', 'tensor'), may hold values from -0.1875 to 0.1875
- w_out: bfloat16 [4304, 1152], P('tensor', 'fsdp'), may hold values from -0.09375 to 0.09375
- texts: bfloat16 [8, 3072, 1152], P('dp', ('fsdp', 'tensor')), may hold values from -6 to 6
Outputs:
- grad_pooled: float32 [8, 3072, 1152], P('dp', 'fsdp')
- grad_in: float32 [1152, 4304], P('fsdp', 'tensor')
- grad_out: float32 [4304, 1152], P('tensor', 'fsdp')
All inputs are finite; a program needn't handle non-finite values.
Results may differ from a plain program's by a relative error of at most 0.022.
Values may be sent and summed in bfloat16 or wider, within the bound.
A program may use at most 64 MiB of HBM per device.

v0:
```python
import jax
import jax.numpy as jnp
from jax import lax
from jax.sharding import PartitionSpec as P

ln_eps = 1e-06
norm_eps = 1e-06
logit_scale = 10.0
logit_bias = -2.0


def passed_along(block, axis, distance):
    devices = range(lax.axis_size(axis))
    route = [((i - distance) % len(devices), i) for i in devices]
    return lax.ppermute(block, axis, route)


def gelu_tanh(values):
    return jax.nn.gelu(values, approximate=True)


def unit_rows(values):
    return values / jnp.sqrt(jnp.sum(values * values, axis=-1, keepdims=True) + norm_eps)


def text_columns(first, number, block_rows, offset, stride):
    places = first + jnp.arange(number, dtype=jnp.int32)
    return places // block_rows * stride + offset + places % block_rows


def body(pooled, ln_gain, w_in, w_out, texts):
    rows = pooled[0].astype(jnp.float32)
    images = rows.shape[0]
    width = rows.shape[1]
    row_mean = jnp.mean(rows, axis=1, keepdims=True)
    centred = rows - row_mean
    inv_std = lax.rsqrt(jnp.mean(centred * centred, axis=1, keepdims=True) + ln_eps)
    normal_rows = centred * inv_std
    unit_in = (normal_rows * ln_gain).astype(jnp.bfloat16)
    full_in = lax.all_gather(w_in, "fsdp", axis=0, tiled=True)
    pre_act = jnp.dot(unit_in, full_in, preferred_element_type=jnp.float32)
    hidden = gelu_tanh(pre_act).astype(jnp.bfloat16)
    full_out = lax.all_gather(w_out, "fsdp", axis=1, tiled=True)
    partial_mix = jnp.dot(hidden, full_out, preferred_element_type=jnp.float32)
    mixed = rows + lax.psum(partial_mix.astype(jnp.bfloat16), "tensor").astype(jnp.float32)
    row_norm = jnp.sqrt(jnp.sum(mixed * mixed, axis=1, keepdims=True) + norm_eps)
    image_unit = mixed / row_norm
    image_b = image_unit.astype(jnp.bfloat16)
    text_b = unit_rows(texts[0].astype(jnp.float32)).astype(jnp.bfloat16)
    cycle_index = lax.axis_index("fsdp")
    cycle_size = lax.axis_size("fsdp")
    image_places = cycle_index * images + jnp.arange(images, dtype=jnp.int32)
    offset = lax.axis_index("tensor") * text_b.shape[0]
    block_rows = text_b.shape[0]

    def score_block(running, block, columns):
        logits = (
            logit_scale
            * jnp.einsum("rd,cd->rc", image_b, block, preferred_element_type=jnp.float32)
            + logit_bias
        )
        match = (image_places[:, None] == columns[None, :]).astype(jnp.float32)
        weights = (jax.nn.sigmoid(logits) - match).astype(jnp.bfloat16)
        return running + jnp.dot(weights, block, preferred_element_type=jnp.float32)

    def source_columns(source):
        return text_columns(source * block_rows, block_rows, block_rows, offset, images)

    empty = jnp.zeros((images, width), jnp.float32)
    running = score_block(empty, text_b, source_columns(cycle_index))

    def cycle_turn(turn, carry):
        total, moving = carry
        moving = passed_along(moving, "fsdp", 1)
        total = score_block(total, moving, source_columns((cycle_index - turn) % cycle_size))
        return (total, moving)

    running, _ = lax.fori_loop(1, cycle_size, cycle_turn, (running, text_b))
    grad_unit = logit_scale * running
    grad_unit = lax.psum(grad_unit.astype(jnp.bfloat16), "tensor").astype(jnp.float32)
    grad_mixed = (
        grad_unit - image_unit * jnp.sum(image_unit * grad_unit, axis=1, keepdims=True)
    ) / row_norm
    grad_b = grad_mixed.astype(jnp.bfloat16)
    grad_hidden = jnp.einsum("rd,fd->rf", grad_b, full_out, preferred_element_type=jnp.float32)
    _, gelu_back = jax.vjp(gelu_tanh, pre_act)
    grad_pre = gelu_back(grad_hidden)[0].astype(jnp.bfloat16)
    partial_unit = jnp.einsum("rf,df->rd", grad_pre, full_in, preferred_element_type=jnp.float32)
    grad_unit_in = lax.psum(partial_unit.astype(jnp.bfloat16), "tensor").astype(jnp.float32)
    scaled = grad_unit_in * ln_gain
    grad_rows = inv_std * (
        scaled
        - jnp.mean(scaled, axis=1, keepdims=True)
        - normal_rows * jnp.mean(scaled * normal_rows, axis=1, keepdims=True)
    )
    grad_pooled = (grad_mixed + grad_rows)[None]
    grad_in_part = lax.psum_scatter(
        jnp.einsum("rd,rf->df", unit_in, grad_pre, preferred_element_type=jnp.float32).astype(
            jnp.bfloat16
        ),
        "fsdp",
        scatter_dimension=0,
        tiled=True,
    )
    out_term = jnp.einsum("rf,rd->fd", hidden, grad_b, preferred_element_type=jnp.float32)
    grad_out_part = lax.psum_scatter(
        out_term.astype(jnp.bfloat16), "fsdp", scatter_dimension=1, tiled=True
    )
    grad_in, grad_out = (
        lax.psum(grad_in_part, "dp").astype(jnp.float32),
        lax.psum(grad_out_part, "dp").astype(jnp.float32),
    )
    return (grad_pooled, grad_in, grad_out)


def solution(mesh):
    placed = (
        P("dp", "fsdp", None),
        P(),
        P("fsdp", "tensor"),
        P("tensor", "fsdp"),
        P("dp", ("fsdp", "tensor"), None),
    )
    return jax.shard_map(
        body,
        mesh=mesh,
        in_specs=placed,
        out_specs=(P("dp", "fsdp", None), P("fsdp", "tensor"), P("tensor", "fsdp")),
        check_vma=False,
    )
```

profile of v0, /device:TPU:32, one launch (start us, length us, event | category | flops | bytes accessed | tf_op | source)
XLA Modules:
  0.0 573.5 jit_solution(10789957357336990693)
XLA Ops:
  7.2 0.7 all-gather.3.cloned.1.call-update
  8.0 0.7 all-gather.5.cloned.1.call-update
  8.8 1.1 fusion.53
  9.8 1.2 convert_reduce_fusion
  11.0 1.3 fusion.48
  12.3 42.3 %all-gather.3.cloned.1.call-done = bf16[1152,2152]{1,0:T(8,128)(2,1)} async-done(((bf16[72,2152]{1,0:T(8,128)(2,1)}), bf16[1152,2152]{1,0:T(8,128)(2,1)}) %all-gather.3.cloned.1.call-update) | async-done | bytes 4958224 | tf_op jit(solution)/shard_map/all_gather | solution.py:40
  54.6 3.8 fusion.72
  58.5 39.3 %all-gather.5.cloned.1.call-done = bf16[2152,1152]{0,1:T(8,128)(2,1)} async-done(((bf16[2152,72]{0,1:T(8,128)(2,1)}), bf16[2152,1152]{0,1:T(8,128)(2,1)}) %all-gather.5.cloned.1.call-update) | async-done | bytes 4958224 | tf_op jit(solution)/shard_map/all_gather | solution.py:43
  97.7 4.9 convolution_convert_fusion.3
  102.6 0.0 all-reduce.10.cloned.1.call-start
  102.7 0.1 fusion.54
  102.8 39.1 %all-reduce.8.cloned.1.call-done = bf16[192,1152]{1,0:T(8,128)(2,1)} async-done(((bf16[192,1152]{1,0:T(8,128)(2,1)}), bf16[192,1152]{1,0:T(8,128)(2,1)}) %all-reduce.8.cloned.1.call-update) | async-done | bytes 442384 | tf_op jit(solution)/shard_map/psum | solution.py:45
  142.0 1.2 multiply_reduce_fusion
  143.2 1.2 fusion.74
  144.4 0.7 fusion.34
  145.0 101.4 %while.19 = (s32[]{:T(128)}, f32[192,1152]{1,0:T(8,128)S(1)}, bf16[96,1152]{1,0:T(8,128)(2,1)S(1)}, bf16[192,1152]{1,0:T(8,128)(2,1)S(1)}, s32[]{:T(128)}, /*ind...) while((s32[]{:T(128)}, f32[192,1152]{1,0:T(8,128)S(1)}, ...), condition=%wide.region_6.7_spmd.clone, body=%wide.region_5.6_spmd.clone.sunk | while | flops 85323472 | bytes 3762734 | solution.py:78
  145.1 5.3 collective-permute-done
  150.4 0.7 convolution_add_fusion.2
  151.2 5.3 collective-permute-done
  156.5 0.7 convolution_add_fusion.2
  157.3 5.3 collective-permute-done
  162.6 0.7 convolution_add_fusion.2
  163.4 5.3 collective-permute-done
  168.7 0.7 convolution_add_fusion.2
  169.4 5.3 collective-permute-done
  174.8 0.7 convolution_add_fusion.2
  175.5 5.3 collective-permute-done
  180.8 0.7 convolution_add_fusion.2
  181.6 5.8 %collective-permute-done = bf16[96,1152]{1,0:T(8,128)(2,1)S(1)} collective-permute-done((bf16[96,1152]{1,0:T(8,128)(2,1)S(1)}, bf16[96,1152]{1,0:T(8,128)(2,1)S(1)}, u32[]{:S(2)}, u32[]{:S(2)}) %collective-permute-start) | collective-permute-done | bytes 221216 | tf_op jit(solution)/shard_map/while/body/eval_jaxpr/ppermute | solution.py:15
  187.4 0.7 convolution_add_fusion.2
  188.2 6.5 %collective-permute-done = bf16[96,1152]{1,0:T(8,128)(2,1)S(1)} collective-permute-done((bf16[96,1152]{1,0:T(8,128)(2,1)S(1)}, bf16[96,1152]{1,0:T(8,128)(2,1)S(1)}, u32[]{:S(2)}, u32[]{:S(2)}) %collective-permute-start) | collective-permute-done | bytes 221216 | tf_op jit(solution)/shard_map/while/body/eval_jaxpr/ppermute | solution.py:15
  194.7 0.7 convolution_add_fusion.2
  195.5 6.5 %collective-permute-done = bf16[96,1152]{1,0:T(8,128)(2,1)S(1)} collective-permute-done((bf16[96,1152]{1,0:T(8,128)(2,1)S(1)}, bf16[96,1152]{1,0:T(8,128)(2,1)S(1)}, u32[]{:S(2)}, u32[]{:S(2)}) %collective-permute-start) | collective-permute-done | bytes 221216 | tf_op jit(solution)/shard_map/while/body/eval_jaxpr/ppermute | solution.py:15
  202.0 0.7 convolution_add_fusion.2
  202.8 6.5 %collective-permute-done = bf16[96,1152]{1,0:T(8,128)(2,1)S(1)} collective-permute-done((bf16[96,1152]{1,0:T(8,128)(2,1)S(1)}, bf16[96,1152]{1,0:T(8,128)(2,1)S(1)}, u32[]{:S(2)}, u32[]{:S(2)}) %collective-permute-start) | collective-permute-done | bytes 221216 | tf_op jit(solution)/shard_map/while/body/eval_jaxpr/ppermute | solution.py:15
  209.3 0.7 convolution_add_fusion.2
  210.1 6.5 %collective-permute-done = bf16[96,1152]{1,0:T(8,128)(2,1)S(1)} collective-permute-done((bf16[96,1152]{1,0:T(8,128)(2,1)S(1)}, bf16[96,1152]{1,0:T(8,128)(2,1)S(1)}, u32[]{:S(2)}, u32[]{:S(2)}) %collective-permute-start) | collective-permute-done | bytes 221216 | tf_op jit(solution)/shard_map/while/body/eval_jaxpr/ppermute | solution.py:15
  216.6 0.7 convolution_add_fusion.2
  217.4 6.5 %collective-permute-done = bf16[96,1152]{1,0:T(8,128)(2,1)S(1)} collective-permute-done((bf16[96,1152]{1,0:T(8,128)(2,1)S(1)}, bf16[96,1152]{1,0:T(8,128)(2,1)S(1)}, u32[]{:S(2)}, u32[]{:S(2)}) %collective-permute-start) | collective-permute-done | bytes 221216 | tf_op jit(solution)/shard_map/while/body/eval_jaxpr/ppermute | solution.py:15
  223.9 0.7 convolution_add_fusion.2
  224.7 6.5 %collective-permute-done = bf16[96,1152]{1,0:T(8,128)(2,1)S(1)} collective-permute-done((bf16[96,1152]{1,0:T(8,128)(2,1)S(1)}, bf16[96,1152]{1,0:T(8,128)(2,1)S(1)}, u32[]{:S(2)}, u32[]{:S(2)}) %collective-permute-start) | collective-permute-done | bytes 221216 | tf_op jit(solution)/shard_map/while/body/eval_jaxpr/ppermute | solution.py:15
  231.2 0.7 convolution_add_fusion.2
  232.0 6.5 %collective-permute-done = bf16[96,1152]{1,0:T(8,128)(2,1)S(1)} collective-permute-done((bf16[96,1152]{1,0:T(8,128)(2,1)S(1)}, bf16[96,1152]{1,0:T(8,128)(2,1)S(1)}, u32[]{:S(2)}, u32[]{:S(2)}) %collective-permute-start) | collective-permute-done | bytes 221216 | tf_op jit(solution)/shard_map/while/body/eval_jaxpr/ppermute | solution.py:15
  238.5 0.7 convolution_add_fusion.2
  239.3 6.5 %collective-permute-done = bf16[96,1152]{1,0:T(8,128)(2,1)S(1)} collective-permute-done((bf16[96,1152]{1,0:T(8,128)(2,1)S(1)}, bf16[96,1152]{1,0:T(8,128)(2,1)S(1)}, u32[]{:S(2)}, u32[]{:S(2)}) %collective-permute-start) | collective-permute-done | bytes 221216 | tf_op jit(solution)/shard_map/while/body/eval_jaxpr/ppermute | solution.py:15
  245.8 0.7 convolution_add_fusion.2
  246.5 0.8 multiply_convert_fusion.1
  247.3 0.0 all-reduce.12.cloned.1.call-start
  247.4 47.6 %all-reduce.10.cloned.1.call-done = bf16[192,1152]{1,0:T(8,128)(2,1)} async-done(((bf16[192,1152]{1,0:T(8,128)(2,1)}), bf16[192,1152]{1,0:T(8,128)(2,1)}) %all-reduce.10.cloned.1.call-update) | async-done | bytes 442384 | tf_op jit(solution)/shard_map/psum | solution.py:80
  294.9 1.5 fusion.49
  296.4 4.7 fusion.26
  301.2 2.4 convolution_convert_fusion.2
  303.7 3.9 convolution_convert_fusion.1
  307.6 0.2 reduce-scatter.9.cloned.1.call-start
  307.9 0.8 copy-done.3
  308.6 4.1 convolution_convert_fusion
  312.8 30.4 %all-reduce.12.cloned.1.call-done = bf16[192,1152]{1,0:T(8,128)(2,1)} async-done(((bf16[192,1152]{1,0:T(8,128)(2,1)}), bf16[192,1152]{1,0:T(8,128)(2,1)}) %all-reduce.12.cloned.1.call-update) | async-done | bytes 442384 | tf_op jit(solution)/shard_map/psum | solution.py:89
  343.3 1.4 fusion.51
  344.7 64.2 %reduce-scatter.7.cloned.1.call-done = bf16[72,2152]{1,0:T(8,128)(2,1)} async-done(((bf16[1152,2152]{1,0:T(8,128)(2,1)}), bf16[72,2152]{1,0:T(8,128)(2,1)}) %reduce-scatter.7.cloned.1.call-update) | async-done | bytes 309904
  408.9 68.5 %reduce-scatter.9.cloned.1.call-done = bf16[2152,72]{0,1:T(8,128)(2,1)} async-done(((bf16[2152,1152]{0,1:T(8,128)(2,1)}), bf16[2152,72]{0,1:T(8,128)(2,1)}) %reduce-scatter.9.cloned.1.call-update) | async-done | bytes 309904
  477.4 1.5 fusion.47
  478.9 84.1 %all-reduce.14.cloned.1.call-done = (bf16[72,2152]{1,0:T(8,128)(2,1)}, bf16[2152,72]{0,1:T(8,128)(2,1)}) async-done(((bf16[72,2152]{1,0:T(8,128)(2,1)}, bf16[2152,72]{0,1:T(8,128)(2,1)}), (bf16[72,2152]{1,0:T(8,128)(2,1)}, bf16[2152,72]{0,1:T(8,128)(2,1)})) %all-reduce.14.cloned.1.call-update) | async-done | bytes 619792 | tf_op jit(solution)/shard_map/psum | solution.py:110
  563.0 1.8 convert_element_type.107
  564.9 1.8 convert_element_type.109
  (98 shorter events, 1.4 us)
Async XLA Ops:
  7.2 47.5 %copy-start = (bf16[1,192,1152]{2,1,0:T(8,128)(2,1)S(1)}, bf16[1,192,1152]{2,1,0:T(8,128)(2,1)}, u32[]{:S(2)}) copy-start(bf16[1,192,1152]{2,1,0:T(8,128)(2,1)} %param.7) | copy-start | bytes 1327108
  7.2 47.5 %copy-start.7 = (f32[1152]{0:T(1024)S(1)}, f32[1152]{0:T(1024)}, u32[]{:S(2)}) copy-start(f32[1152]{0:T(1024)} %param.8) | copy-start | bytes 13828
  7.2 47.4 %all-gather.3.cloned.1.call-start = ((), (), s32[]{:S(2)}) async-start(), calls=%async_computation.2 | async-start | bytes 5326848 | tf_op jit(solution)/shard_map/all_gather | solution.py:40
  7.9 89.8 %all-gather.5.cloned.1.call-start = ((), (), s32[]{:S(2)}) async-start(), calls=%async_computation.3 | async-start | bytes 5326848 | tf_op jit(solution)/shard_map/all_gather | solution.py:43
  8.7 133.3 %all-reduce.8.cloned.1.call-start = ((), (), s32[]{:S(2)}) async-start(), calls=%async_computation.4 | async-start | bytes 884736 | tf_op jit(solution)/shard_map/psum | solution.py:45
  58.4 44.2 %copy-start.4 = (f32[192,2152]{1,0:T(8,128)}, f32[192,2152]{1,0:T(8,128)S(1)}, u32[]{:S(2)}) copy-start(f32[192,2152]{1,0:T(8,128)S(1)} %fusion.72) | copy-start | bytes 4958212
  58.5 44.2 %copy-start.6 = (bf16[1,96,1152]{2,1,0:T(8,128)(2,1)S(1)}, bf16[1,96,1152]{2,1,0:T(8,128)(2,1)}, u32[]{:S(2)}) copy-start(bf16[1,96,1152]{2,1,0:T(8,128)(2,1)} %param.11) | copy-start | bytes 663556
  102.6 192.3 %all-reduce.10.cloned.1.call-start = ((), (), s32[]{:S(2)}) async-start(), calls=%async_computation.5 | async-start | bytes 884736 | tf_op jit(solution)/shard_map/psum | solution.py:80
  145.0 5.4 collective-permute-start
  151.1 5.4 collective-permute-start
  157.2 5.4 collective-permute-start
  163.3 5.4 collective-permute-start
  169.4 5.4 collective-permute-start
  175.4 5.4 collective-permute-start
  181.5 5.9 %collective-permute-start = (bf16[96,1152]{1,0:T(8,128)(2,1)S(1)}, bf16[96,1152]{1,0:T(8,128)(2,1)S(1)}, u32[]{:S(2)}, u32[]{:S(2)}) collective-permute-start(bf16[96,1152]{1,0:T(8,128)(2,1)S(1)} %get-tuple-element.306), channel_id=1, source_target_pairs={{30,0},{0,2},{2,4},{4,6},{6,8},{8,10},{10,12},{12,14},{14,16},{16,... | collective-permute-start | bytes 663560 | tf_op jit(solution)/shard_map/while/body/eval_jaxpr/ppermute | solution.py:15
  188.1 6.6 %collective-permute-start = (bf16[96,1152]{1,0:T(8,128)(2,1)S(1)}, bf16[96,1152]{1,0:T(8,128)(2,1)S(1)}, u32[]{:S(2)}, u32[]{:S(2)}) collective-permute-start(bf16[96,1152]{1,0:T(8,128)(2,1)S(1)} %get-tuple-element.306), channel_id=1, source_target_pairs={{30,0},{0,2},{2,4},{4,6},{6,8},{8,10},{10,12},{12,14},{14,16},{16,... | collective-permute-start | bytes 663560 | tf_op jit(solution)/shard_map/while/body/eval_jaxpr/ppermute | solution.py:15
  195.4 6.6 %collective-permute-start = (bf16[96,1152]{1,0:T(8,128)(2,1)S(1)}, bf16[96,1152]{1,0:T(8,128)(2,1)S(1)}, u32[]{:S(2)}, u32[]{:S(2)}) collective-permute-start(bf16[96,1152]{1,0:T(8,128)(2,1)S(1)} %get-tuple-element.306), channel_id=1, source_target_pairs={{30,0},{0,2},{2,4},{4,6},{6,8},{8,10},{10,12},{12,14},{14,16},{16,... | collective-permute-start | bytes 663560 | tf_op jit(solution)/shard_map/while/body/eval_jaxpr/ppermute | solution.py:15
  202.7 6.6 %collective-permute-start = (bf16[96,1152]{1,0:T(8,128)(2,1)S(1)}, bf16[96,1152]{1,0:T(8,128)(2,1)S(1)}, u32[]{:S(2)}, u32[]{:S(2)}) collective-permute-start(bf16[96,1152]{1,0:T(8,128)(2,1)S(1)} %get-tuple-element.306), channel_id=1, source_target_pairs={{30,0},{0,2},{2,4},{4,6},{6,8},{8,10},{10,12},{12,14},{14,16},{16,... | collective-permute-start | bytes 663560 | tf_op jit(solution)/shard_map/while/body/eval_jaxpr/ppermute | solution.py:15
  210.0 6.6 %collective-permute-start = (bf16[96,1152]{1,0:T(8,128)(2,1)S(1)}, bf16[96,1152]{1,0:T(8,128)(2,1)S(1)}, u32[]{:S(2)}, u32[]{:S(2)}) collective-permute-start(bf16[96,1152]{1,0:T(8,128)(2,1)S(1)} %get-tuple-element.306), channel_id=1, source_target_pairs={{30,0},{0,2},{2,4},{4,6},{6,8},{8,10},{10,12},{12,14},{14,16},{16,... | collective-permute-start | bytes 663560 | tf_op jit(solution)/shard_map/while/body/eval_jaxpr/ppermute | solution.py:15
  217.3 6.6 %collective-permute-start = (bf16[96,1152]{1,0:T(8,128)(2,1)S(1)}, bf16[96,1152]{1,0:T(8,128)(2,1)S(1)}, u32[]{:S(2)}, u32[]{:S(2)}) collective-permute-start(bf16[96,1152]{1,0:T(8,128)(2,1)S(1)} %get-tuple-element.306), channel_id=1, source_target_pairs={{30,0},{0,2},{2,4},{4,6},{6,8},{8,10},{10,12},{12,14},{14,16},{16,... | collective-permute-start | bytes 663560 | tf_op jit(solution)/shard_map/while/body/eval_jaxpr/ppermute | solution.py:15
  224.6 6.6 %collective-permute-start = (bf16[96,1152]{1,0:T(8,128)(2,1)S(1)}, bf16[96,1152]{1,0:T(8,128)(2,1)S(1)}, u32[]{:S(2)}, u32[]{:S(2)}) collective-permute-start(bf16[96,1152]{1,0:T(8,128)(2,1)S(1)} %get-tuple-element.306), channel_id=1, source_target_pairs={{30,0},{0,2},{2,4},{4,6},{6,8},{8,10},{10,12},{12,14},{14,16},{16,... | collective-permute-start | bytes 663560 | tf_op jit(solution)/shard_map/while/body/eval_jaxpr/ppermute | solution.py:15
  231.9 6.6 %collective-permute-start = (bf16[96,1152]{1,0:T(8,128)(2,1)S(1)}, bf16[96,1152]{1,0:T(8,128)(2,1)S(1)}, u32[]{:S(2)}, u32[]{:S(2)}) collective-permute-start(bf16[96,1152]{1,0:T(8,128)(2,1)S(1)} %get-tuple-element.306), channel_id=1, source_target_pairs={{30,0},{0,2},{2,4},{4,6},{6,8},{8,10},{10,12},{12,14},{14,16},{16,... | collective-permute-start | bytes 663560 | tf_op jit(solution)/shard_map/while/body/eval_jaxpr/ppermute | solution.py:15
  239.2 6.6 %collective-permute-start = (bf16[96,1152]{1,0:T(8,128)(2,1)S(1)}, bf16[96,1152]{1,0:T(8,128)(2,1)S(1)}, u32[]{:S(2)}, u32[]{:S(2)}) collective-permute-start(bf16[96,1152]{1,0:T(8,128)(2,1)S(1)} %get-tuple-element.306), channel_id=1, source_target_pairs={{30,0},{0,2},{2,4},{4,6},{6,8},{8,10},{10,12},{12,14},{14,16},{16,... | collective-permute-start | bytes 663560 | tf_op jit(solution)/shard_map/while/body/eval_jaxpr/ppermute | solution.py:15
  246.5 48.5 %copy-start.1 = (bf16[192,1152]{1,0:T(8,128)(2,1)S(1)}, bf16[192,1152]{1,0:T(8,128)(2,1)}, u32[]{:S(2)}) copy-start(bf16[192,1152]{1,0:T(8,128)(2,1)} %all-reduce.8.cloned.1.call-done) | copy-start | bytes 1327108
  246.5 49.9 %copy-start.5 = (f32[192,2152]{1,0:T(8,128)S(1)}, f32[192,2152]{1,0:T(8,128)}, u32[]{:S(2)}) copy-start(f32[192,2152]{1,0:T(8,128)} %copy-done.4) | copy-start | bytes 4958212
  247.3 95.9 %all-reduce.12.cloned.1.call-start = ((), (), s32[]{:S(2)}) async-start(), calls=%async_computation.6 | async-start | bytes 884736 | tf_op jit(solution)/shard_map/psum | solution.py:89
  294.9 6.2 %slice-start = ((s8[5013504]{0:T(1024)(128)(4,1)}), s8[4194304]{0:T(1024)(128)(4,1)S(1)}, s32[]{:S(2)}) async-start(s8[5013504]{0:T(1024)(128)(4,1)} %bitcast.75), calls=%async_computation.10 | async-start | bytes 8388608
  296.4 4.8 slice-start.1
  303.6 105.3 %reduce-scatter.7.cloned.1.call-start = ((), (), s32[]{:S(2)}) async-start(), calls=%async_computation.7 | async-start | bytes 5326848
  307.6 1.0 copy-start.3
  307.6 169.8 %reduce-scatter.9.cloned.1.call-start = ((), (), s32[]{:S(2)}) async-start(), calls=%async_computation.8 | async-start | bytes 5326848
  312.8 250.3 %all-reduce.14.cloned.1.call-start = ((), (), s32[]{:S(2)}) async-start(), calls=%async_computation.9 | async-start | bytes 1253376 | tf_op jit(solution)/shard_map/psum | solution.py:110
  343.3 134.2 %copy-start.2 = (bf16[192,1152]{1,0:T(8,128)(2,1)S(1)}, bf16[192,1152]{1,0:T(8,128)(2,1)}, u32[]{:S(2)}) copy-start(bf16[192,1152]{1,0:T(8,128)(2,1)} %all-reduce.12.cloned.1.call-done) | copy-start | bytes 1327108
Sparse Core Ops, SparseCore 0:
  9.8 44.7 all-gather.2
  56.5 41.2 all-gather.4
  102.8 39.1 all-reduce.7
  247.4 47.4 all-reduce.9
  303.7 39.4 all-reduce.11
  345.7 63.1 reduce-scatter.6
  411.5 65.8 reduce-scatter.8
  480.1 82.8 all-reduce.13
where the time goes:
time: 574 us
  waiting for transfers between devices  507 us (88%)
  matrix products  34.6 us (6%)
  other arithmetic  15.3 us (3%)
  between operations  14.3 us (2%)
    unnamed x10, waiting for transfers between devices  134 us
    ppermute x15, waiting for transfers between devices, passed_along(): return lax.ppermute(block, axis, route)  89.5 us
    psum x1, waiting for transfers between devices, body(): lax.psum(grad_in_part, 'dp').astype(jnp.float32)  84.1 us
    psum x1, waiting for transfers between devices, body(): lax.psum(grad_unit.astype(jnp.bfloat16), 'tensor').astype(jnp.float32)  47.6 us
    all_gather x1, waiting for transfers between devices, body(): full_in = lax.all_gather(w_in, 'fsdp', axis=0, tiled=True)  42.3 us
    all_gather x1, waiting for transfers between devices, body(): full_out = lax.all_gather(w_out, 'fsdp', axis=1, tiled=True)  39.3 us
    psum x1, waiting for transfers between devices, body(): lax.psum(partial_mix.astype(jnp.bfloat16), 'tensor').astype(jnp.float32)  39.1 us
    psum x1, waiting for transfers between devices, body(): lax.psum(partial_unit.astype(jnp.bfloat16), 'tensor').astype(jnp.float32)  30.4 us
  transfers between devices with their start and end apart: 23, of which 23 were waited for; matrix products, arithmetic and copies ran while one was open for 3% of the time, Pallas kernels for 0%

commit v1 on v0

--- a/solution.py
+++ b/solution.py
@@ -1,3 +1,4 @@
+import functools
 import jax
 import jax.numpy as jnp
 from jax import lax
@@ -7,6 +8,13 @@
 norm_eps = 1e-06
 logit_scale = 10.0
 logit_bias = -2.0
+
+
+def wait_vectors(xx, comm_axis):
+    return lax.all_gather(xx, comm_axis).sum(axis=0)
+
+
+_check_racks = functools.partial(wait_vectors, comm_axis="tensor")
 
 
 def passed_along(block, axis, distance):
@@ -86,7 +94,7 @@
     _, gelu_back = jax.vjp(gelu_tanh, pre_act)
     grad_pre = gelu_back(grad_hidden)[0].astype(jnp.bfloat16)
     partial_unit = jnp.einsum("rf,df->rd", grad_pre, full_in, preferred_element_type=jnp.float32)
-    grad_unit_in = lax.psum(partial_unit.astype(jnp.bfloat16), "tensor").astype(jnp.float32)
+    grad_unit_in = _check_racks(partial_unit.astype(jnp.bfloat16)).astype(jnp.float32)
     scaled = grad_unit_in * ln_gain
     grad_rows = inv_std * (
         scaled

time: 574 us -> 533 us (0.929)
  waiting for transfers between devices: 507 us -> 450 us
  blocking collectives: 0 us -> 13.9 us
    psum x1 -> x0, waiting for transfers between devices: 30.4 us -> none  [body(): lax.psum(partial_unit.astype(jnp.bfloat16), 'tensor').astype(jnp.float32)]
    unnamed x10 -> x9, waiting for transfers between devices: 134 us -> 108 us
    all_gather x0 -> x1, blocking collectives: none -> 13.9 us  [wait_vectors(): return lax.all_gather(xx, comm_axis).sum(axis=0)]
  transfers between devices with their start and end apart: 23 -> 22, of which waited for: 23 -> 22; matrix products, arithmetic and copies ran while one was open for 3% -> 3% of each run, Pallas kernels for 0% -> 0%
where the time goes in v1:
time: 533 us
  waiting for transfers between devices  450 us (84%)
  matrix products  36.3 us (7%)
  other arithmetic  14.4 us (3%)
  between operations  14.3 us (3%)
  blocking collectives  13.9 us (3%)
    unnamed x9, waiting for transfers between devices  108 us
    ppermute x15, waiting for transfers between devices, passed_along(): return lax.ppermute(block, axis, route)  89.5 us
    psum x1, waiting for transfers between devices, body(): lax.psum(grad_in_part, 'dp').astype(jnp.float32)  84 us
    psum x1, waiting for transfers between devices, body(): lax.psum(grad_unit.astype(jnp.bfloat16), 'tensor').astype(jnp.float32)  47.6 us
    all_gather x1, waiting for transfers between devices, body(): full_in = lax.all_gather(w_in, 'fsdp', axis=0, tiled=True)  42.3 us
    all_gather x1, waiting for transfers between devices, body(): full_out = lax.all_gather(w_out, 'fsdp', axis=1, tiled=True)  39.3 us
    psum x1, waiting for transfers between devices, body(): lax.psum(partial_mix.astype(jnp.bfloat16), 'tensor').astype(jnp.float32)  39.1 us
    all_gather x1, blocking collectives, wait_vectors(): return lax.all_gather(xx, comm_axis).sum(axis=0)  13.9 us
  transfers between devices with their start and end apart: 22, of which 22 were waited for; matrix products, arithmetic and copies ran while one was open for 3% of the time, Pallas kernels for 0%

profile of v1, /device:TPU:32, one launch (start us, length us, event | category | flops | bytes accessed | tf_op | source)
XLA Modules:
  0.0 532.9 jit_solution(7388615795490596390)
XLA Ops:
  7.2 0.7 all-gather.4.cloned.1.call-update
  8.0 0.7 all-gather.6.cloned.1.call-update
  8.8 1.1 fusion.53
  9.8 1.2 convert_reduce_fusion
  11.0 1.3 fusion.48
  12.3 42.3 %all-gather.4.cloned.1.call-done = bf16[1152,2152]{1,0:T(8,128)(2,1)} async-done(((bf16[72,2152]{1,0:T(8,128)(2,1)}), bf16[1152,2152]{1,0:T(8,128)(2,1)}) %all-gather.4.cloned.1.call-update) | async-done | bytes 4958224 | tf_op jit(solution)/shard_map/all_gather | solution.py:48
  54.6 3.8 fusion.72
  58.5 39.3 %all-gather.6.cloned.1.call-done = bf16[2152,1152]{0,1:T(8,128)(2,1)} async-done(((bf16[2152,72]{0,1:T(8,128)(2,1)}), bf16[2152,1152]{0,1:T(8,128)(2,1)}) %all-gather.6.cloned.1.call-update) | async-done | bytes 4958224 | tf_op jit(solution)/shard_map/all_gather | solution.py:51
  97.7 4.9 convolution_convert_fusion.3
  102.7 0.1 fusion.54
  102.8 39.1 %all-reduce.7.cloned.1.call-done = bf16[192,1152]{1,0:T(8,128)(2,1)} async-done(((bf16[192,1152]{1,0:T(8,128)(2,1)}), bf16[192,1152]{1,0:T(8,128)(2,1)}) %all-reduce.7.cloned.1.call-update) | async-done | bytes 442384 | tf_op jit(solution)/shard_map/psum | solution.py:53
  142.0 1.2 multiply_reduce_fusion
  143.2 1.2 fusion.74
  144.4 0.7 fusion.34
  145.0 101.4 %while.19 = (s32[]{:T(128)}, f32[192,1152]{1,0:T(8,128)S(1)}, bf16[96,1152]{1,0:T(8,128)(2,1)S(1)}, bf16[192,1152]{1,0:T(8,128)(2,1)S(1)}, s32[]{:T(128)}, /*ind...) while((s32[]{:T(128)}, f32[192,1152]{1,0:T(8,128)S(1)}, ...), condition=%wide.region_6.7_spmd.clone, body=%wide.region_5.6_spmd.clone.sunk | while | flops 85323472 | bytes 3762734 | solution.py:86
  145.1 5.3 collective-permute-done
  150.4 0.7 convolution_add_fusion.2
  151.2 5.3 collective-permute-done
  156.5 0.7 convolution_add_fusion.2
  157.3 5.3 collective-permute-done
  162.6 0.7 convolution_add_fusion.2
  163.4 5.3 collective-permute-done
  168.7 0.7 convolution_add_fusion.2
  169.4 5.3 collective-permute-done
  174.8 0.7 convolution_add_fusion.2
  175.5 5.3 collective-permute-done
  180.8 0.7 convolution_add_fusion.2
  181.6 5.8 %collective-permute-done = bf16[96,1152]{1,0:T(8,128)(2,1)S(1)} collective-permute-done((bf16[96,1152]{1,0:T(8,128)(2,1)S(1)}, bf16[96,1152]{1,0:T(8,128)(2,1)S(1)}, u32[]{:S(2)}, u32[]{:S(2)}) %collective-permute-start) | collective-permute-done | bytes 221216 | tf_op jit(solution)/shard_map/while/body/eval_jaxpr/ppermute | solution.py:23
  187.4 0.7 convolution_add_fusion.2
  188.2 6.5 %collective-permute-done = bf16[96,1152]{1,0:T(8,128)(2,1)S(1)} collective-permute-done((bf16[96,1152]{1,0:T(8,128)(2,1)S(1)}, bf16[96,1152]{1,0:T(8,128)(2,1)S(1)}, u32[]{:S(2)}, u32[]{:S(2)}) %collective-permute-start) | collective-permute-done | bytes 221216 | tf_op jit(solution)/shard_map/while/body/eval_jaxpr/ppermute | solution.py:23
  194.7 0.7 convolution_add_fusion.2
  195.5 6.5 %collective-permute-done = bf16[96,1152]{1,0:T(8,128)(2,1)S(1)} collective-permute-done((bf16[96,1152]{1,0:T(8,128)(2,1)S(1)}, bf16[96,1152]{1,0:T(8,128)(2,1)S(1)}, u32[]{:S(2)}, u32[]{:S(2)}) %collective-permute-start) | collective-permute-done | bytes 221216 | tf_op jit(solution)/shard_map/while/body/eval_jaxpr/ppermute | solution.py:23
  202.0 0.7 convolution_add_fusion.2
  202.8 6.5 %collective-permute-done = bf16[96,1152]{1,0:T(8,128)(2,1)S(1)} collective-permute-done((bf16[96,1152]{1,0:T(8,128)(2,1)S(1)}, bf16[96,1152]{1,0:T(8,128)(2,1)S(1)}, u32[]{:S(2)}, u32[]{:S(2)}) %collective-permute-start) | collective-permute-done | bytes 221216 | tf_op jit(solution)/shard_map/while/body/eval_jaxpr/ppermute | solution.py:23
  209.3 0.7 convolution_add_fusion.2
  210.1 6.5 %collective-permute-done = bf16[96,1152]{1,0:T(8,128)(2,1)S(1)} collective-permute-done((bf16[96,1152]{1,0:T(8,128)(2,1)S(1)}, bf16[96,1152]{1,0:T(8,128)(2,1)S(1)}, u32[]{:S(2)}, u32[]{:S(2)}) %collective-permute-start) | collective-permute-done | bytes 221216 | tf_op jit(solution)/shard_map/while/body/eval_jaxpr/ppermute | solution.py:23
  216.6 0.7 convolution_add_fusion.2
  217.4 6.5 %collective-permute-done = bf16[96,1152]{1,0:T(8,128)(2,1)S(1)} collective-permute-done((bf16[96,1152]{1,0:T(8,128)(2,1)S(1)}, bf16[96,1152]{1,0:T(8,128)(2,1)S(1)}, u32[]{:S(2)}, u32[]{:S(2)}) %collective-permute-start) | collective-permute-done | bytes 221216 | tf_op jit(solution)/shard_map/while/body/eval_jaxpr/ppermute | solution.py:23
  223.9 0.7 convolution_add_fusion.2
  224.7 6.5 %collective-permute-done = bf16[96,1152]{1,0:T(8,128)(2,1)S(1)} collective-permute-done((bf16[96,1152]{1,0:T(8,128)(2,1)S(1)}, bf16[96,1152]{1,0:T(8,128)(2,1)S(1)}, u32[]{:S(2)}, u32[]{:S(2)}) %collective-permute-start) | collective-permute-done | bytes 221216 | tf_op jit(solution)/shard_map/while/body/eval_jaxpr/ppermute | solution.py:23
  231.2 0.7 convolution_add_fusion.2
  232.0 6.5 %collective-permute-done = bf16[96,1152]{1,0:T(8,128)(2,1)S(1)} collective-permute-done((bf16[96,1152]{1,0:T(8,128)(2,1)S(1)}, bf16[96,1152]{1,0:T(8,128)(2,1)S(1)}, u32[]{:S(2)}, u32[]{:S(2)}) %collective-permute-start) | collective-permute-done | bytes 221216 | tf_op jit(solution)/shard_map/while/body/eval_jaxpr/ppermute | solution.py:23
  238.5 0.7 convolution_add_fusion.2
  239.3 6.5 %collective-permute-done = bf16[96,1152]{1,0:T(8,128)(2,1)S(1)} collective-permute-done((bf16[96,1152]{1,0:T(8,128)(2,1)S(1)}, bf16[96,1152]{1,0:T(8,128)(2,1)S(1)}, u32[]{:S(2)}, u32[]{:S(2)}) %collective-permute-start) | collective-permute-done | bytes 221216 | tf_op jit(solution)/shard_map/while/body/eval_jaxpr/ppermute | solution.py:23
  245.8 0.7 convolution_add_fusion.2
  246.5 0.8 multiply_convert_fusion.1
  247.4 47.6 %all-reduce.9.cloned.1.call-done = bf16[192,1152]{1,0:T(8,128)(2,1)} async-done(((bf16[192,1152]{1,0:T(8,128)(2,1)}), bf16[192,1152]{1,0:T(8,128)(2,1)}) %all-reduce.9.cloned.1.call-update) | async-done | bytes 442384 | tf_op jit(solution)/shard_map/psum | solution.py:88
  294.9 1.3 fusion.49
  296.3 4.7 fusion.26
  301.0 4.0 convolution_convert_fusion.1
  305.0 0.9 copy-done.2
  306.0 4.2 convolution_convert_fusion
  310.2 0.2 all-reduce.11.cloned.1.call-start
  310.4 0.9 copy-done.7
  311.3 4.0 convolution_convert_fusion.2
  315.4 13.9 %all-gather = bf16[384,1152]{1,0:T(8,128)(2,1)S(1)} all-gather(bf16[192,1152]{1,0:T(8,128)(2,1)S(1)} %convolution_convert_fusion.2), channel_id=2, replica_groups=mesh['dp'=8,'fsdp'=16,'tensor'=2] {'tensor'}, dimensions={0}, use_global_device_ids=true | all-gather | bytes 1327104 | tf_op jit(solution)/shard_map/all_gather | solution.py:14
  329.3 0.2 reduce_sum.80
  329.5 0.3 fusion.51
  329.9 38.7 %reduce-scatter.7.cloned.1.call-done = bf16[72,2152]{1,0:T(8,128)(2,1)} async-done(((bf16[1152,2152]{1,0:T(8,128)(2,1)}), bf16[72,2152]{1,0:T(8,128)(2,1)}) %reduce-scatter.7.cloned.1.call-update) | async-done | bytes 309904
  368.6 68.3 %reduce-scatter.9.cloned.1.call-done = bf16[2152,72]{0,1:T(8,128)(2,1)} async-done(((bf16[2152,1152]{0,1:T(8,128)(2,1)}), bf16[2152,72]{0,1:T(8,128)(2,1)}) %reduce-scatter.9.cloned.1.call-update) | async-done | bytes 309904
  436.9 1.5 fusion.47
  438.3 84.0 %all-reduce.11.cloned.1.call-done = (bf16[72,2152]{1,0:T(8,128)(2,1)}, bf16[2152,72]{0,1:T(8,128)(2,1)}) async-done(((bf16[72,2152]{1,0:T(8,128)(2,1)}, bf16[2152,72]{0,1:T(8,128)(2,1)}), (bf16[72,2152]{1,0:T(8,128)(2,1)}, bf16[2152,72]{0,1:T(8,128)(2,1)})) %all-reduce.11.cloned.1.call-update) | async-done | bytes 619792 | tf_op jit(solution)/shard_map/psum | solution.py:118
  522.4 1.8 convert_element_type.109
  524.2 1.8 convert_element_type.111
  (94 shorter events, 1.4 us)
Async XLA Ops:
  7.2 47.5 %copy-start = (bf16[1,192,1152]{2,1,0:T(8,128)(2,1)S(1)}, bf16[1,192,1152]{2,1,0:T(8,128)(2,1)}, u32[]{:S(2)}) copy-start(bf16[1,192,1152]{2,1,0:T(8,128)(2,1)} %param.7) | copy-start | bytes 1327108
  7.2 47.5 %copy-start.8 = (f32[1152]{0:T(1024)S(1)}, f32[1152]{0:T(1024)}, u32[]{:S(2)}) copy-start(f32[1152]{0:T(1024)} %param.8) | copy-start | bytes 13828
  7.2 47.4 %all-gather.4.cloned.1.call-start = ((), (), s32[]{:S(2)}) async-start(), calls=%async_computation.2 | async-start | bytes 5326848 | tf_op jit(solution)/shard_map/all_gather | solution.py:48
  7.9 89.8 %all-gather.6.cloned.1.call-start = ((), (), s32[]{:S(2)}) async-start(), calls=%async_computation.3 | async-start | bytes 5326848 | tf_op jit(solution)/shard_map/all_gather | solution.py:51
  8.7 133.3 %all-reduce.7.cloned.1.call-start = ((), (), s32[]{:S(2)}) async-start(), calls=%async_computation.4 | async-start | bytes 884736 | tf_op jit(solution)/shard_map/psum | solution.py:53
  58.4 44.2 %copy-start.3 = (f32[192,2152]{1,0:T(8,128)}, f32[192,2152]{1,0:T(8,128)S(1)}, u32[]{:S(2)}) copy-start(f32[192,2152]{1,0:T(8,128)S(1)} %fusion.72) | copy-start | bytes 4958212
  58.5 44.2 %copy-start.5 = (bf16[1,96,1152]{2,1,0:T(8,128)(2,1)S(1)}, bf16[1,96,1152]{2,1,0:T(8,128)(2,1)}, u32[]{:S(2)}) copy-start(bf16[1,96,1152]{2,1,0:T(8,128)(2,1)} %param.11) | copy-start | bytes 663556
  102.6 192.3 %all-reduce.9.cloned.1.call-start = ((), (), s32[]{:S(2)}) async-start(), calls=%async_computation.5 | async-start | bytes 884736 | tf_op jit(solution)/shard_map/psum | solution.py:88
  145.0 5.4 %collective-permute-start = (bf16[96,1152]{1,0:T(8,128)(2,1)S(1)}, bf16[96,1152]{1,0:T(8,128)(2,1)S(1)}, u32[]{:S(2)}, u32[]{:S(2)}) collective-permute-start(bf16[96,1152]{1,0:T(8,128)(2,1)S(1)} %get-tuple-element.306), channel_id=1, source_target_pairs={{30,0},{0,2},{2,4},{4,6},{6,8},{8,10},{10,12},{12,14},{14,16},{16,... | collective-permute-start | bytes 663560 | tf_op jit(solution)/shard_map/while/body/eval_jaxpr/ppermute | solution.py:23
  151.1 5.4 %collective-permute-start = (bf16[96,1152]{1,0:T(8,128)(2,1)S(1)}, bf16[96,1152]{1,0:T(8,128)(2,1)S(1)}, u32[]{:S(2)}, u32[]{:S(2)}) collective-permute-start(bf16[96,1152]{1,0:T(8,128)(2,1)S(1)} %get-tuple-element.306), channel_id=1, source_target_pairs={{30,0},{0,2},{2,4},{4,6},{6,8},{8,10},{10,12},{12,14},{14,16},{16,... | collective-permute-start | bytes 663560 | tf_op jit(solution)/shard_map/while/body/eval_jaxpr/ppermute | solution.py:23
  157.2 5.4 %collective-permute-start = (bf16[96,1152]{1,0:T(8,128)(2,1)S(1)}, bf16[96,1152]{1,0:T(8,128)(2,1)S(1)}, u32[]{:S(2)}, u32[]{:S(2)}) collective-permute-start(bf16[96,1152]{1,0:T(8,128)(2,1)S(1)} %get-tuple-element.306), channel_id=1, source_target_pairs={{30,0},{0,2},{2,4},{4,6},{6,8},{8,10},{10,12},{12,14},{14,16},{16,... | collective-permute-start | bytes 663560 | tf_op jit(solution)/shard_map/while/body/eval_jaxpr/ppermute | solution.py:23
  163.3 5.4 %collective-permute-start = (bf16[96,1152]{1,0:T(8,128)(2,1)S(1)}, bf16[96,1152]{1,0:T(8,128)(2,1)S(1)}, u32[]{:S(2)}, u32[]{:S(2)}) collective-permute-start(bf16[96,1152]{1,0:T(8,128)(2,1)S(1)} %get-tuple-element.306), channel_id=1, source_target_pairs={{30,0},{0,2},{2,4},{4,6},{6,8},{8,10},{10,12},{12,14},{14,16},{16,... | collective-permute-start | bytes 663560 | tf_op jit(solution)/shard_map/while/body/eval_jaxpr/ppermute | solution.py:23
  169.4 5.4 %collective-permute-start = (bf16[96,1152]{1,0:T(8,128)(2,1)S(1)}, bf16[96,1152]{1,0:T(8,128)(2,1)S(1)}, u32[]{:S(2)}, u32[]{:S(2)}) collective-permute-start(bf16[96,1152]{1,0:T(8,128)(2,1)S(1)} %get-tuple-element.306), channel_id=1, source_target_pairs={{30,0},{0,2},{2,4},{4,6},{6,8},{8,10},{10,12},{12,14},{14,16},{16,... | collective-permute-start | bytes 663560 | tf_op jit(solution)/shard_map/while/body/eval_jaxpr/ppermute | solution.py:23
  175.4 5.4 %collective-permute-start = (bf16[96,1152]{1,0:T(8,128)(2,1)S(1)}, bf16[96,1152]{1,0:T(8,128)(2,1)S(1)}, u32[]{:S(2)}, u32[]{:S(2)}) collective-permute-start(bf16[96,1152]{1,0:T(8,128)(2,1)S(1)} %get-tuple-element.306), channel_id=1, source_target_pairs={{30,0},{0,2},{2,4},{4,6},{6,8},{8,10},{10,12},{12,14},{14,16},{16,... | collective-permute-start | bytes 663560 | tf_op jit(solution)/shard_map/while/body/eval_jaxpr/ppermute | solution.py:23
  181.5 5.9 %collective-permute-start = (bf16[96,1152]{1,0:T(8,128)(2,1)S(1)}, bf16[96,1152]{1,0:T(8,128)(2,1)S(1)}, u32[]{:S(2)}, u32[]{:S(2)}) collective-permute-start(bf16[96,1152]{1,0:T(8,128)(2,1)S(1)} %get-tuple-element.306), channel_id=1, source_target_pairs={{30,0},{0,2},{2,4},{4,6},{6,8},{8,10},{10,12},{12,14},{14,16},{16,... | collective-permute-start | bytes 663560 | tf_op jit(solution)/shard_map/while/body/eval_jaxpr/ppermute | solution.py:23
  188.1 6.6 %collective-permute-start = (bf16[96,1152]{1,0:T(8,128)(2,1)S(1)}, bf16[96,1152]{1,0:T(8,128)(2,1)S(1)}, u32[]{:S(2)}, u32[]{:S(2)}) collective-permute-start(bf16[96,1152]{1,0:T(8,128)(2,1)S(1)} %get-tuple-element.306), channel_id=1, source_target_pairs={{30,0},{0,2},{2,4},{4,6},{6,8},{8,10},{10,12},{12,14},{14,16},{16,... | collective-permute-start | bytes 663560 | tf_op jit(solution)/shard_map/while/body/eval_jaxpr/ppermute | solution.py:23
  195.4 6.6 %collective-permute-start = (bf16[96,1152]{1,0:T(8,128)(2,1)S(1)}, bf16[96,1152]{1,0:T(8,128)(2,1)S(1)}, u32[]{:S(2)}, u32[]{:S(2)}) collective-permute-start(bf16[96,1152]{1,0:T(8,128)(2,1)S(1)} %get-tuple-element.306), channel_id=1, source_target_pairs={{30,0},{0,2},{2,4},{4,6},{6,8},{8,10},{10,12},{12,14},{14,16},{16,... | collective-permute-start | bytes 663560 | tf_op jit(solution)/shard_map/while/body/eval_jaxpr/ppermute | solution.py:23
  202.7 6.6 %collective-permute-start = (bf16[96,1152]{1,0:T(8,128)(2,1)S(1)}, bf16[96,1152]{1,0:T(8,128)(2,1)S(1)}, u32[]{:S(2)}, u32[]{:S(2)}) collective-permute-start(bf16[96,1152]{1,0:T(8,128)(2,1)S(1)} %get-tuple-element.306), channel_id=1, source_target_pairs={{30,0},{0,2},{2,4},{4,6},{6,8},{8,10},{10,12},{12,14},{14,16},{16,... | collective-permute-start | bytes 663560 | tf_op jit(solution)/shard_map/while/body/eval_jaxpr/ppermute | solution.py:23
  210.0 6.6 %collective-permute-start = (bf16[96,1152]{1,0:T(8,128)(2,1)S(1)}, bf16[96,1152]{1,0:T(8,128)(2,1)S(1)}, u32[]{:S(2)}, u32[]{:S(2)}) collective-permute-start(bf16[96,1152]{1,0:T(8,128)(2,1)S(1)} %get-tuple-element.306), channel_id=1, source_target_pairs={{30,0},{0,2},{2,4},{4,6},{6,8},{8,10},{10,12},{12,14},{14,16},{16,... | collective-permute-start | bytes 663560 | tf_op jit(solution)/shard_map/while/body/eval_jaxpr/ppermute | solution.py:23
  217.3 6.6 %collective-permute-start = (bf16[96,1152]{1,0:T(8,128)(2,1)S(1)}, bf16[96,1152]{1,0:T(8,128)(2,1)S(1)}, u32[]{:S(2)}, u32[]{:S(2)}) collective-permute-start(bf16[96,1152]{1,0:T(8,128)(2,1)S(1)} %get-tuple-element.306), channel_id=1, source_target_pairs={{30,0},{0,2},{2,4},{4,6},{6,8},{8,10},{10,12},{12,14},{14,16},{16,... | collective-permute-start | bytes 663560 | tf_op jit(solution)/shard_map/while/body/eval_jaxpr/ppermute | solution.py:23
  224.6 6.6 %collective-permute-start = (bf16[96,1152]{1,0:T(8,128)(2,1)S(1)}, bf16[96,1152]{1,0:T(8,128)(2,1)S(1)}, u32[]{:S(2)}, u32[]{:S(2)}) collective-permute-start(bf16[96,1152]{1,0:T(8,128)(2,1)S(1)} %get-tuple-element.306), channel_id=1, source_target_pairs={{30,0},{0,2},{2,4},{4,6},{6,8},{8,10},{10,12},{12,14},{14,16},{16,... | collective-permute-start | bytes 663560 | tf_op jit(solution)/shard_map/while/body/eval_jaxpr/ppermute | solution.py:23
  231.9 6.6 %collective-permute-start = (bf16[96,1152]{1,0:T(8,128)(2,1)S(1)}, bf16[96,1152]{1,0:T(8,128)(2,1)S(1)}, u32[]{:S(2)}, u32[]{:S(2)}) collective-permute-start(bf16[96,1152]{1,0:T(8,128)(2,1)S(1)} %get-tuple-element.306), channel_id=1, source_target_pairs={{30,0},{0,2},{2,4},{4,6},{6,8},{8,10},{10,12},{12,14},{14,16},{16,... | collective-permute-start | bytes 663560 | tf_op jit(solution)/shard_map/while/body/eval_jaxpr/ppermute | solution.py:23
  239.2 6.6 %collective-permute-start = (bf16[96,1152]{1,0:T(8,128)(2,1)S(1)}, bf16[96,1152]{1,0:T(8,128)(2,1)S(1)}, u32[]{:S(2)}, u32[]{:S(2)}) collective-permute-start(bf16[96,1152]{1,0:T(8,128)(2,1)S(1)} %get-tuple-element.306), channel_id=1, source_target_pairs={{30,0},{0,2},{2,4},{4,6},{6,8},{8,10},{10,12},{12,14},{14,16},{16,... | collective-permute-start | bytes 663560 | tf_op jit(solution)/shard_map/while/body/eval_jaxpr/ppermute | solution.py:23
  246.5 48.5 %copy-start.1 = (bf16[192,1152]{1,0:T(8,128)(2,1)S(1)}, bf16[192,1152]{1,0:T(8,128)(2,1)}, u32[]{:S(2)}) copy-start(bf16[192,1152]{1,0:T(8,128)(2,1)} %all-reduce.7.cloned.1.call-done) | copy-start | bytes 1327108
  246.5 49.8 %copy-start.4 = (f32[192,2152]{1,0:T(8,128)S(1)}, f32[192,2152]{1,0:T(8,128)}, u32[]{:S(2)}) copy-start(f32[192,2152]{1,0:T(8,128)} %copy-done.3) | copy-start | bytes 4958212
  247.3 121.2 %reduce-scatter.7.cloned.1.call-start = ((), (), s32[]{:S(2)}) async-start(), calls=%async_computation.6 | async-start | bytes 5326848
  300.9 4.0 copy-start.6
  305.0 1.0 copy-start.2
  305.0 131.8 %reduce-scatter.9.cloned.1.call-start = ((), (), s32[]{:S(2)}) async-start(), calls=%async_computation.7 | async-start | bytes 5326848
  310.2 1.1 copy-start.7
  310.2 212.1 %all-reduce.11.cloned.1.call-start = ((), (), s32[]{:S(2)}) async-start(), calls=%async_computation.8 | async-start | bytes 1253376 | tf_op jit(solution)/shard_map/psum | solution.py:118
Sparse Core Ops, SparseCore 0:
  9.8 44.7 all-gather.3
  56.5 41.2 all-gather.5
  102.8 39.1 all-reduce.6
  247.4 47.4 all-reduce.8
  305.1 63.3 reduce-scatter.6
  371.0 65.8 reduce-scatter.8
  439.6 82.7 all-reduce.10
